TPU v7x, 32 devices: a whole 2x2x4 slice. The times are simulated.
32 devices in a mesh: grp: 2 (over x), tok: 4 (over y, core), feat: 4 (over z).
Axes of the slice: x: 2, y: 2, z: 4, core: 2. Of those that a mesh axis runs over, the one named last changes fastest.
Arguments:
- activations: bfloat16 [4096, 3072], P(('grp', 'tok', 'feat')), parts along dimension 0, may hold values from -6 to 6
- block_lists: int32 [2048, 4], P(('grp', 'tok', 'feat')), parts along dimension 0, may hold values from 0 to 15, as said below
- top_positions: int32 [4096, 64], P(('grp', 'tok', 'feat')), parts along dimension 0, may hold values from 0 to 2047, as said below
- enc_weight: bfloat16 [3072, 8192], P(None, ('tok', 'feat')), may hold values from -0.109375 to 0.109375
- enc_bias: float32 [8192], P(('tok', 'feat')), may hold values from -3 to 3
- dec_weight: bfloat16 [8192, 3072], P(('tok', 'feat')), may hold values from -2.5 to 2.5
- dec_bias: float32 [3072], replicated, may hold values from -6 to 6
Outputs:
- enc_grad: bfloat16 [3072, 16384], P(None, ('grp', 'tok', 'feat')), parts along dimension 1
- dec_grad: bfloat16 [16384, 3072], P(('grp', 'tok', 'feat')), parts along dimension 0
There are 2 independent parts, one for each index of `grp`. A program takes and returns all parts, laid end to end along the dimension named above; an argument that names none is the same for every part. Nothing has to cross between parts.
Inputs may be any that keep to these rules, and one draw needn't show every extreme that they name: `block_lists`: each row block names 4 different feature blocks. In the aligned blocks of 64 rows that one device holds, no feature block is named more than 24 times. In every draw one feature block is named exactly 24 times in every such block of rows. `top_positions`: the 64 entries of a token are distinct.
All inputs are finite; a program needn't handle non-finite values.
Results may differ from a plain program's by a relative error of at most 0.0058.
Values may be sent and summed in bfloat16 or wider, within the bound.
A program may use at most 128 MiB of HBM per device.

v0:
```python
import jax
import jax.numpy as jnp
from jax import lax
from jax.sharding import PartitionSpec as P


def dispatch_rows(send_x, send_rel):
    result = (
        lax.all_to_all(send_x, ("tok", "feat"), split_axis=0, concat_axis=0, tiled=True),
        lax.all_to_all(send_rel, ("tok", "feat"), split_axis=0, concat_axis=0, tiled=True),
    )
    return result


def return_partials(partial_value):
    result = lax.all_to_all(partial_value, ("tok", "feat"), split_axis=0, concat_axis=0, tiled=True)
    return result


def dispatch_errors(send_err):
    result = lax.all_to_all(send_err, ("tok", "feat"), split_axis=0, concat_axis=0, tiled=True)
    return result


def routed_plan(
    activations, block_lists, top_positions, enc_weight, enc_bias, dec_weight, dec_bias
):
    owner_count = lax.axis_size(("tok", "feat"))
    token_count, model_width = activations.shape
    block_rows, active_count = block_lists.shape
    group_rows = token_count // block_rows
    feat_block = enc_weight.shape[1]
    top_count = top_positions.shape[1]
    slot_count = max(2, 3 * token_count * active_count // (2 * group_rows * owner_count))
    per_owner = slot_count * group_rows
    buffer_rows = owner_count * per_owner
    pair_count = block_rows * active_count
    pair_ids = block_lists.reshape(pair_count)
    pair_order = jnp.arange(pair_count, dtype=jnp.int32)
    earlier = (pair_ids[:, None] == pair_ids[None, :]) & (pair_order[None, :] < pair_order[:, None])
    pair_rank = jnp.sum(earlier.astype(jnp.int32), axis=1)
    lane_index = jnp.arange(group_rows, dtype=jnp.int32)
    target = (
        (pair_ids * per_owner + pair_rank * group_rows)[:, None] + lane_index[None, :]
    ).reshape(-1)
    source = ((pair_order // active_count * group_rows)[:, None] + lane_index[None, :]).reshape(-1)
    column = jnp.repeat(pair_order % active_count, group_rows)
    slot_index = jnp.arange(buffer_rows, dtype=jnp.int32)
    hit_bool = slot_index[:, None] == target[None, :]
    hit_float = hit_bool.astype(jnp.float32)
    place_float = jnp.sum(
        hit_float.reshape(buffer_rows, block_rows, active_count, group_rows), axis=2
    ).reshape(buffer_rows, token_count)
    place = place_float.astype(jnp.bfloat16)
    filled = jnp.sum(place_float, axis=1)
    send_x = jnp.dot(place, activations, preferred_element_type=jnp.float32).astype(jnp.bfloat16)
    offsets = top_positions[source] - column[:, None] * feat_block
    offsets = jnp.where((offsets >= 0) & (offsets < feat_block), offsets, feat_block)
    rel_float = (
        jnp.dot(hit_float, offsets.astype(jnp.float32), precision=lax.Precision.HIGHEST)
        + (1.0 - filled)[:, None] * feat_block
    )
    send_rel = rel_float.astype(jnp.int32)
    recv_x, recv_rel = dispatch_rows(
        send_x.reshape(owner_count, per_owner, model_width),
        send_rel.reshape(owner_count, per_owner, top_count),
    )
    recv_x = recv_x.reshape(buffer_rows, model_width)
    recv_rel = recv_rel.reshape(buffer_rows, top_count)
    feature_iota = jnp.arange(feat_block, dtype=jnp.int32)
    mask_bool = jnp.zeros((buffer_rows, feat_block), jnp.bool_)
    for begin in range(0, top_count, 8):
        piece = recv_rel[:, begin : begin + 8]
        mask_bool = mask_bool | jnp.any(piece[:, :, None] == feature_iota[None, None, :], axis=1)
    feat_mask = mask_bool.astype(jnp.float32)
    pre_acts = jnp.dot(recv_x, enc_weight, preferred_element_type=jnp.float32) + enc_bias
    code_vals = (feat_mask * pre_acts).astype(jnp.bfloat16)
    partial_value = jnp.dot(code_vals, dec_weight, preferred_element_type=jnp.float32).astype(
        jnp.bfloat16
    )
    returned = return_partials(partial_value.reshape(owner_count, per_owner, model_width)).reshape(
        buffer_rows, model_width
    )
    summed = lax.dot_general(
        place, returned, (((0,), (0,)), ((), ())), preferred_element_type=jnp.float32
    )
    residual = (summed + dec_bias - activations.astype(jnp.float32)).astype(jnp.bfloat16)
    send_err = jnp.dot(place, residual, preferred_element_type=jnp.float32).astype(jnp.bfloat16)
    recv_err = dispatch_errors(send_err.reshape(owner_count, per_owner, model_width)).reshape(
        buffer_rows, model_width
    )
    grad_codes = lax.dot_general(
        recv_err, dec_weight, (((1,), (1,)), ((), ())), preferred_element_type=jnp.float32
    )
    grad_pre = (feat_mask * grad_codes).astype(jnp.bfloat16)
    enc_grad = lax.dot_general(
        recv_x, grad_pre, (((0,), (0,)), ((), ())), preferred_element_type=jnp.float32
    ).astype(jnp.bfloat16)
    raw_grad = lax.dot_general(
        code_vals, recv_err, (((0,), (0,)), ((), ())), preferred_element_type=jnp.float32
    )
    dec_float = dec_weight.astype(jnp.float32)
    along_coef = jnp.sum(raw_grad * dec_float, axis=1) / (
        jnp.sum(dec_float * dec_float, axis=1) + 1e-06
    )
    dec_grad = (raw_grad - along_coef[:, None] * dec_float).astype(jnp.bfloat16)
    return (enc_grad, dec_grad)


GROUP = ("tok", "feat")


def global_ids(block_lists, top_positions, feat_block):
    token_count = top_positions.shape[0]
    block_rows, active_count = block_lists.shape
    lists = jnp.repeat(block_lists, token_count // block_rows, axis=0)
    column = top_positions // feat_block
    chosen = jnp.zeros_like(top_positions)
    for k in range(active_count):
        chosen = jnp.where(column == k, lists[:, k : k + 1], chosen)
    return chosen * feat_block + top_positions % feat_block


def select_mask(rel, feat_block):
    words = feat_block // 8
    inside = (rel >= 0) & (rel < feat_block)
    word = jnp.where(inside, rel // 8, words)
    bit = jnp.left_shift(1, rel & 7)
    word_iota = jnp.arange(words, dtype=jnp.int32)
    packed = jnp.sum(
        jnp.where(word[:, :, None] == word_iota[None, None, :], bit[:, :, None], 0), axis=1
    )
    feature_iota = jnp.arange(feat_block, dtype=jnp.int32)
    spread = (word_iota[:, None] == (feature_iota // 8)[None, :]).astype(jnp.bfloat16)
    wide = jnp.dot(
        packed.astype(jnp.float32).astype(jnp.bfloat16), spread, preferred_element_type=jnp.float32
    ).astype(jnp.int32)
    return (jnp.right_shift(wide, (feature_iota & 7)[None, :]) & 1).astype(jnp.bfloat16)


def gathered_plan(
    activations, block_lists, top_positions, enc_weight, enc_bias, dec_weight, dec_bias
):
    feat_block = enc_weight.shape[1]
    ids = global_ids(block_lists, top_positions, feat_block)
    all_ids = lax.all_gather(ids, GROUP, axis=0, tiled=True)
    all_x = lax.all_gather(activations, GROUP, axis=0, tiled=True)
    mask = select_mask(all_ids - lax.axis_index(GROUP) * feat_block, feat_block)
    pre_acts = jnp.dot(all_x, enc_weight, preferred_element_type=jnp.float32) + enc_bias
    code_vals = jnp.where(mask > 0, pre_acts, 0.0).astype(jnp.bfloat16)
    partial_value = jnp.dot(code_vals, dec_weight, preferred_element_type=jnp.float32).astype(
        jnp.bfloat16
    )
    summed = lax.psum_scatter(partial_value, GROUP, scatter_dimension=0, tiled=True)
    residual = (summed.astype(jnp.float32) + dec_bias - activations.astype(jnp.float32)).astype(
        jnp.bfloat16
    )
    all_err = lax.all_gather(residual, GROUP, axis=0, tiled=True)
    grad_codes = lax.dot_general(
        all_err, dec_weight, (((1,), (1,)), ((), ())), preferred_element_type=jnp.float32
    )
    grad_pre = jnp.where(mask > 0, grad_codes, 0.0).astype(jnp.bfloat16)
    enc_grad = lax.dot_general(
        all_x, grad_pre, (((0,), (0,)), ((), ())), preferred_element_type=jnp.float32
    ).astype(jnp.bfloat16)
    raw_grad = lax.dot_general(
        code_vals, all_err, (((0,), (0,)), ((), ())), preferred_element_type=jnp.float32
    )
    dec_float = dec_weight.astype(jnp.float32)
    along_coef = jnp.sum(raw_grad * dec_float, axis=1) / (
        jnp.sum(dec_float * dec_float, axis=1) + 1e-06
    )
    dec_grad = (raw_grad - along_coef[:, None] * dec_float).astype(jnp.bfloat16)
    return (enc_grad, dec_grad)


def on_device(activations, block_lists, top_positions, *weights):
    owner_count = lax.axis_size(GROUP)
    pairs = activations.shape[0] * block_lists.shape[1]
    gathered = owner_count * activations.shape[0]
    if gathered <= 4 * pairs:
        return gathered_plan(activations, block_lists, top_positions, *weights)
    return routed_plan(activations, block_lists, top_positions, *weights)


def solution(mesh):
    placed = (
        P(("grp", "tok", "feat"), None),
        P(("grp", "tok", "feat"), None),
        P(("grp", "tok", "feat"), None),
        P(None, ("tok", "feat")),
        P(("tok", "feat")),
        P(("tok", "feat"), None),
        P(),
    )
    return jax.shard_map(
        on_device,
        mesh=mesh,
        in_specs=placed,
        out_specs=(P(None, ("grp", "tok", "feat")), P(("grp", "tok", "feat"), None)),
        check_vma=False,
    )
```

profile of v0, /device:TPU:0, one launch (start us, length us, event | category | flops | bytes accessed | tf_op | source)
XLA Modules:
  0.0 425.1 jit_solution(17819520309938272814)
XLA Ops:
  7.2 0.0 copy-start
  7.2 0.0 all-gather.3.cloned.1.call-start
  7.2 0.7 all-gather.3.cloned.1.call-update
  7.9 0.0 reduce-scatter.2.cloned.1.call-start
  8.0 0.9 copy.20
  8.9 0.2 slice_reduce_fusion.3
  9.2 0.8 fusion.11
  10.0 45.2 %all_gather.9 = s32[2048,64]{0,1:T(8,128)S(1)} all-gather(s32[128,64]{0,1:T(8,128)S(1)} %fusion.11), channel_id=1, replica_groups=mesh['grp'=2,'tok'=4,'feat'=4] {'tok','feat'}, dimensions={0}, use_global_device_ids=true | all-gather | bytes 557056 | tf_op jit(solution)/shard_map/all_gather | solution.py:146
  55.2 0.4 fusion.8
  55.6 8.9 %select_reduce_fusion = s32[2048,64]{0,1:T(8,128)S(1)} fusion(s32[2048,64]{0,1:T(8,128)S(1)} %get-tuple-element.17, s32[2048,64]{0,1:T(8,128)S(1)} %get-tuple-element.16), kind=kLoop, calls=%fused_computation | loop fusion | flops 25034752 | bytes 1572864 | tf_op jit(solution)/shard_map/reduce_sum | solution.py:130
  64.5 0.0 copy-start.6
  64.6 2.5 fusion.5
  67.0 54.2 %all-gather.3.cloned.1.call-done = bf16[2048,3072]{1,0:T(8,128)(2,1)} async-done(((bf16[128,3072]{1,0:T(8,128)(2,1)}), bf16[2048,3072]{1,0:T(8,128)(2,1)}) %all-gather.3.cloned.1.call-update) | async-done | bytes 12582928 | tf_op jit(solution)/shard_map/all_gather | solution.py:147
  121.2 0.0 copy-done
  121.2 0.0 copy-done.6
  121.2 0.0 copy-start.3
  121.2 10.1 %select_convert_fusion.1 = bf16[2048,512]{1,0:T(8,128)(2,1)S(1)} fusion(pred[2048,512]{1,0:T(32,128)(4,1)} %fusion.5, bf16[2048,3072]{1,0:T(8,128)(2,1)} %all-gather.3.cloned.1.call-done, bf16[3072,512]{1,0:T(8,128)(2,1)S(1)} %copy-done, f32[512]{0:T(512)S(1)} %copy-done.6), kind=kOutput, calls=%fused_computation.12 | convolution fusion | flops 6445596672 | bytes 18876416 | tf_op jit(solution)/shard_map/dot_general | solution.py:149
  131.3 0.0 copy-start.7
  131.3 1.3 copy-done.7
  132.6 0.0 copy-done.3
  132.6 9.7 %convolution_convert_fusion = bf16[2048,3072]{1,0:T(8,128)(2,1)} fusion(bf16[2048,512]{1,0:T(8,128)(2,1)S(1)} %select_convert_fusion.1, bf16[512,3072]{1,0:T(8,128)(2,1)S(1)} %copy-done.3), kind=kOutput, calls=%fused_computation.2 | convolution fusion | flops 6448742400 | bytes 17825792 | tf_op jit(solution)/shard_map/dot_general | solution.py:151
  142.4 0.0 copy-start.2
  142.4 0.0 copy-start.5
  142.4 0.0 reduce-scatter.2.cloned.1.call-update
  142.4 0.0 all-gather.5.cloned.1.call-start
  142.5 133.0 %reduce-scatter.2.cloned.1.call-done = bf16[128,3072]{1,0:T(8,128)(2,1)} async-done(((bf16[2048,3072]{1,0:T(8,128)(2,1)}), bf16[128,3072]{1,0:T(8,128)(2,1)}) %reduce-scatter.2.cloned.1.call-update) | async-done | bytes 786448 | tf_op jit(solution)/shard_map/reduce_scatter | solution.py:154
  275.5 0.0 copy-done.2
  275.5 0.0 copy-done.5
  275.5 2.3 subtract_convert_fusion
  277.8 0.0 all-gather.5.cloned.1.call-update
  277.8 100.1 %all-gather.5.cloned.1.call-done = bf16[2048,3072]{1,0:T(8,128)(2,1)} async-done(((bf16[128,3072]{1,0:T(8,128)(2,1)}), bf16[2048,3072]{1,0:T(8,128)(2,1)}) %all-gather.5.cloned.1.call-update) | async-done | bytes 12582928 | tf_op jit(solution)/shard_map/all_gather | solution.py:158
  377.9 23.1 %fusion.4 = bf16[3072,512]{0,1:T(8,128)(2,1)S(1)} fusion(bf16[2048,3072]{1,0:T(8,128)(2,1)} %all-gather.3.cloned.1.call-done, pred[2048,512]{1,0:T(32,128)(4,1)} %fusion.5, bf16[2048,3072]{1,0:T(8,128)(2,1)} %all-gather.5.cloned.1.call-done, bf16[512,3072]{1,0:T(8,128)(2,1)} %param.12), kind=kOutput, calls=%fused_computation.14 | convolution fusion | flops 12888571904 | bytes 32505856 | tf_op jit(solution)/shard_map/dot_general | solution.py:163
  401.0 2.8 copy.21
  403.8 0.0 copy-start.4
  403.8 11.7 %fusion.1 = (f32[512]{0:T(512)S(1)}, f32[512]{0:T(512)S(1)}, f32[512,3072]{1,0:T(8,128)S(1)}) fusion(bf16[512,3072]{1,0:T(8,128)(2,1)} %param.12, bf16[2048,512]{1,0:T(8,128)(2,1)} %copy-done.7, bf16[2048,3072]{1,0:T(8,128)(2,1)} %all-gather.5.cloned.1.call-done), kind=kOutput, calls=%fused_computation.7 | convolution fusion | flops 6450314240 | bytes 24121344 | tf_op jit(solution)/shard_map/dot_general | solution.py:166
  415.5 0.0 copy-start.1
  415.5 0.0 copy-done.4
  415.5 3.1 fusion.3
  418.6 0.0 copy-done.1
  (3 shorter events, 0.0 us)
Async XLA Ops:
  7.2 114.0 %copy-start = (bf16[3072,512]{1,0:T(8,128)(2,1)S(1)}, bf16[3072,512]{1,0:T(8,128)(2,1)}, u32[]{:S(2)}) copy-start(bf16[3072,512]{1,0:T(8,128)(2,1)} %param.10) | copy-start | bytes 9437188
  7.2 114.0 %all-gather.3.cloned.1.call-start = ((), (), s32[]{:S(2)}) async-start(), calls=%async_computation.1 | async-start | bytes 13369344 | tf_op jit(solution)/shard_map/all_gather | solution.py:147
  7.9 267.6 %reduce-scatter.2.cloned.1.call-start = ((), (), s32[]{:S(2)}) async-start(), calls=%async_computation.2 | async-start | bytes 13369344 | tf_op jit(solution)/shard_map/reduce_scatter | solution.py:154
  64.5 56.7 %copy-start.6 = (f32[512]{0:T(512)S(1)}, f32[512]{0:T(512)}, u32[]{:S(2)}) copy-start(f32[512]{0:T(512)} %param.11) | copy-start | bytes 6148
  121.2 11.4 %copy-start.3 = (bf16[512,3072]{1,0:T(8,128)(2,1)S(1)}, bf16[512,3072]{1,0:T(8,128)(2,1)}, u32[]{:S(2)}) copy-start(bf16[512,3072]{1,0:T(8,128)(2,1)} %param.12) | copy-start | bytes 9437188
  131.3 1.3 copy-start.7
  142.4 133.1 %copy-start.2 = (bf16[128,3072]{1,0:T(8,128)(2,1)S(1)}, bf16[128,3072]{1,0:T(8,128)(2,1)}, u32[]{:S(2)}) copy-start(bf16[128,3072]{1,0:T(8,128)(2,1)} %param.7) | copy-start | bytes 2359300
  142.4 133.1 %copy-start.5 = (f32[3072]{0:T(1024)S(1)}, f32[3072]{0:T(1024)}, u32[]{:S(2)}) copy-start(f32[3072]{0:T(1024)} %param.13) | copy-start | bytes 36868
  142.4 235.5 %all-gather.5.cloned.1.call-start = ((), (), s32[]{:S(2)}) async-start(), calls=%async_computation.3 | async-start | bytes 13369344 | tf_op jit(solution)/shard_map/all_gather | solution.py:158
  403.8 11.7 %copy-start.4 = (bf16[512,3072]{1,0:T(8,128)(2,1)S(1)}, bf16[512,3072]{1,0:T(8,128)(2,1)}, u32[]{:S(2)}) copy-start(bf16[512,3072]{1,0:T(8,128)(2,1)} %param.12) | copy-start | bytes 9437188
  415.5 3.1 copy-start.1
Sparse Core Ops, SparseCore 0:
  10.3 110.8 all-gather.2
  142.5 132.9 reduce-scatter.1
  277.9 99.8 all-gather.4
where the time goes:
time: 425 us
  waiting for transfers between devices  288 us (68%)
  matrix products  57.1 us (13%)
  blocking collectives  45.2 us (11%)
  other arithmetic  15.5 us (4%)
  between operations  13.8 us (3%)
  local copies, waits for them, and re-layouts  5.31 us (1%)
    reduce_scatter x1, waiting for transfers between devices, gathered_plan(): lax.psum_scatter(partial_value, GROUP, scatter_dimension=0, tiled=True)  133 us
    all_gather x1, waiting for transfers between devices, gathered_plan(): all_err = lax.all_gather(residual, GROUP, axis=0, tiled=True)  100 us
    all_gather x1, waiting for transfers between devices, gathered_plan(): all_x = lax.all_gather(activations, GROUP, axis=0, tiled=True)  54.2 us
    all_gather x1, blocking collectives, gathered_plan(): all_ids = lax.all_gather(ids, GROUP, axis=0, tiled=True)  45.2 us
    dot_general x1, matrix products, gathered_plan(): lax.dot_general(all_x, grad_pre, (((0,), (0,)), ((), ())), preferred_elem...  23.1 us
    dot_general x1, matrix products, gathered_plan(): lax.dot_general(code_vals, all_err, (((0,), (0,)), ((), ())), preferred_e...  11.7 us
    dot_general x1, matrix products, gathered_plan(): jnp.dot(all_x, enc_weight, preferred_element_type=jnp.float32) + enc_bias  10.1 us
    dot_general x1, matrix products, gathered_plan(): jnp.dot(code_vals, dec_weight, preferred_element_type=jnp.float32)  9.73 us
  transfers between devices with their start and end apart: 3, of which 3 were waited for; matrix products, arithmetic and copies ran while one was open for 3% of the time, Pallas kernels for 0%

commit v1 on v0

--- a/solution.py
+++ b/solution.py
@@ -2,6 +2,12 @@
 import jax.numpy as jnp
 from jax import lax
 from jax.sharding import PartitionSpec as P
+
+
+def draw_quotas_all(local_values, k_dim):
+    after = list(local_values.shape[1:])
+    after[k_dim] *= local_values.shape[0]
+    return jnp.moveaxis(local_values, 0, k_dim).reshape(after)
 
 
 def dispatch_rows(send_x, send_rel):
@@ -144,7 +150,19 @@
     feat_block = enc_weight.shape[1]
     ids = global_ids(block_lists, top_positions, feat_block)
     all_ids = lax.all_gather(ids, GROUP, axis=0, tiled=True)
-    all_x = lax.all_gather(activations, GROUP, axis=0, tiled=True)
+    n_axis = lax.axis_size(GROUP)
+    table = tuple(((p, (p + 1) % n_axis) for p in range(n_axis)))
+    heap = tuple(((nth, k0) for k0, nth in table))
+    inter, clean = ([], [])
+    for num in range(n_axis - 1):
+        if num % 2 == 0:
+            inter.append(lax.ppermute(inter[-1] if inter else activations, GROUP, table))
+        else:
+            clean.append(lax.ppermute(clean[-1] if clean else activations, GROUP, heap))
+    all_values = jnp.stack([*inter[::-1], activations, *clean], axis=0)
+    far_arr = lax.axis_index(GROUP) - len(inter)
+    all_values = all_values[(jnp.arange(n_axis) - far_arr) % n_axis]
+    all_x = draw_quotas_all(all_values, 0)
     mask = select_mask(all_ids - lax.axis_index(GROUP) * feat_block, feat_block)
     pre_acts = jnp.dot(all_x, enc_weight, preferred_element_type=jnp.float32) + enc_bias
     code_vals = jnp.where(mask > 0, pre_acts, 0.0).astype(jnp.bfloat16)

time: 425 us -> 631 us (1.48)
  waiting for transfers between devices: 288 us -> 418 us
  local copies, waits for them, and re-layouts: 5.31 us -> 40.3 us
  starting transfers between devices: 0.12 us -> 18.2 us
  blocking collectives: 45.2 us -> 60.7 us
    ppermute x0 -> x15, waiting for transfers between devices: none -> 183 us  [the longest x8 114 us: gathered_plan(): lax.ppermute(inter[-1] if inter else activations, GROUP, table)]
    all_gather x1 -> x0, waiting for transfers between devices: 54.2 us -> none  [gathered_plan(): all_x = lax.all_gather(activations, GROUP, axis=0, tiled=True)]
    unnamed x18 -> x58, local copies, waits for them, and re-layouts: 5.06 us -> 28 us
    ppermute x0 -> x15, starting transfers between devices: none -> 18.1 us  [the longest x7 13.7 us: gathered_plan(): clean.append(lax.ppermute(clean[-1] if clean else activations, GROUP, heap))]
    all_gather x1, blocking collectives: 45.2 us -> 60.7 us  [gathered_plan(): all_ids = lax.all_gather(ids, GROUP, axis=0, tiled=True)]
    gather x0 -> x1, local copies, waits for them, and re-layouts: none -> 11.1 us  [gathered_plan(): all_values = all_values[(jnp.arange(n_axis) - far_arr) % n_axis]]
  transfers between devices with their start and end apart: 3 -> 17, of which waited for: 3 -> 14; matrix products, arithmetic and copies ran while one was open for 3% -> 6% of each run, Pallas kernels for 0% -> 0%
where the time goes in v1:
time: 631 us; the launch traced here: 628 us
  waiting for transfers between devices  418 us (66%)
  blocking collectives  60.7 us (10%)
  matrix products  60.1 us (10%)
  local copies, waits for them, and re-layouts  40.3 us (6%)
  starting transfers between devices  18.2 us (3%)
  other arithmetic  16.3 us (3%)
  between operations  14.4 us (2%)
    reduce_scatter x1, waiting for transfers between devices, gathered_plan(): lax.psum_scatter(partial_value, GROUP, scatter_dimension=0, tiled=True)  135 us
    ppermute x8, waiting for transfers between devices, gathered_plan(): lax.ppermute(inter[-1] if inter else activations, GROUP, table)  114 us
    all_gather x1, waiting for transfers between devices, gathered_plan(): all_err = lax.all_gather(residual, GROUP, axis=0, tiled=True)  101 us
    ppermute x7, waiting for transfers between devices, gathered_plan(): clean.append(lax.ppermute(clean[-1] if clean else activations, GROUP, heap))  68.6 us
    all_gather x1, blocking collectives, gathered_plan(): all_ids = lax.all_gather(ids, GROUP, axis=0, tiled=True)  60.7 us
    unnamed x58, local copies, waits for them, and re-layouts  28 us
    dot_general x1, matrix products, gathered_plan(): lax.dot_general(all_x, grad_pre, (((0,), (0,)), ((), ())), preferred_elem...  25 us
    ppermute x7, starting transfers between devices, gathered_plan(): clean.append(lax.ppermute(clean[-1] if clean else activations, GROUP, heap))  13.7 us
  transfers between devices with their start and end apart: 17, of which 14 were waited for; matrix products, arithmetic and copies ran while one was open for 6% of the time, Pallas kernels for 0%

profile of v1, /device:TPU:0, one launch (start us, length us, event | category | flops | bytes accessed | tf_op | source)
XLA Modules:
  0.0 628.2 jit_solution(17576451533079092559)
XLA Ops:
  7.2 3.1 collective-permute-start
  10.3 19.9 %collective-permute-done = bf16[128,3072]{1,0:T(8,128)(2,1)S(1)} collective-permute-done((bf16[128,3072]{1,0:T(8,128)(2,1)}, bf16[128,3072]{1,0:T(8,128)(2,1)S(1)}, u32[]{:S(2)}, u32[]{:S(2)}) %collective-permute-start) | collective-permute-done | bytes 786464 | tf_op jit(solution)/shard_map/ppermute | solution.py:159
  30.2 0.9 copy-done.6
  31.1 4.4 collective-permute-start.8
  35.6 18.0 %collective-permute-done.1 = bf16[128,3072]{1,0:T(8,128)(2,1)S(1)} collective-permute-done((bf16[128,3072]{1,0:T(8,128)(2,1)S(1)}, bf16[128,3072]{1,0:T(8,128)(2,1)S(1)}, u32[]{:S(2)}, u32[]{:S(2)}) %collective-permute-start.1) | collective-permute-done | bytes 786464 | tf_op jit(solution)/shard_map/ppermute | solution.py:159
  53.6 14.2 %collective-permute-done.8 = bf16[128,3072]{1,0:T(8,128)(2,1)S(1)} collective-permute-done((bf16[128,3072]{1,0:T(8,128)(2,1)}, bf16[128,3072]{1,0:T(8,128)(2,1)S(1)}, u32[]{:S(2)}, u32[]{:S(2)}) %collective-permute-start.8) | collective-permute-done | bytes 786464 | tf_op jit(solution)/shard_map/ppermute | solution.py:161
  68.6 2.8 collective-permute-start.9
  71.4 16.0 %collective-permute-done.2 = bf16[128,3072]{1,0:T(8,128)(2,1)S(1)} collective-permute-done((bf16[128,3072]{1,0:T(8,128)(2,1)S(1)}, bf16[128,3072]{1,0:T(8,128)(2,1)S(1)}, u32[]{:S(2)}, u32[]{:S(2)}) %collective-permute-start.2) | collective-permute-done | bytes 786464 | tf_op jit(solution)/shard_map/ppermute | solution.py:159
  87.4 16.8 %collective-permute-done.9 = bf16[128,3072]{1,0:T(8,128)(2,1)S(1)} collective-permute-done((bf16[128,3072]{1,0:T(8,128)(2,1)S(1)}, bf16[128,3072]{1,0:T(8,128)(2,1)S(1)}, u32[]{:S(2)}, u32[]{:S(2)}) %collective-permute-start.9) | collective-permute-done | bytes 786464 | tf_op jit(solution)/shard_map/ppermute | solution.py:161
  105.1 16.1 %collective-permute-done.3 = bf16[128,3072]{1,0:T(8,128)(2,1)S(1)} collective-permute-done((bf16[128,3072]{1,0:T(8,128)(2,1)S(1)}, bf16[128,3072]{1,0:T(8,128)(2,1)S(1)}, u32[]{:S(2)}, u32[]{:S(2)}) %collective-permute-start.3) | collective-permute-done | bytes 786464 | tf_op jit(solution)/shard_map/ppermute | solution.py:159
  121.1 17.7 %collective-permute-done.10 = bf16[128,3072]{1,0:T(8,128)(2,1)} collective-permute-done((bf16[128,3072]{1,0:T(8,128)(2,1)S(1)}, bf16[128,3072]{1,0:T(8,128)(2,1)}, u32[]{:S(2)}, u32[]{:S(2)}) %collective-permute-start.10) | collective-permute-done | bytes 786464 | tf_op jit(solution)/shard_map/ppermute | solution.py:161
  138.8 16.2 %collective-permute-done.4 = bf16[128,3072]{1,0:T(8,128)(2,1)} collective-permute-done((bf16[128,3072]{1,0:T(8,128)(2,1)S(1)}, bf16[128,3072]{1,0:T(8,128)(2,1)}, u32[]{:S(2)}, u32[]{:S(2)}) %collective-permute-start.4) | collective-permute-done | bytes 786464 | tf_op jit(solution)/shard_map/ppermute | solution.py:159
  156.0 16.5 %collective-permute-done.11 = bf16[128,3072]{1,0:T(8,128)(2,1)} collective-permute-done((bf16[128,3072]{1,0:T(8,128)(2,1)}, bf16[128,3072]{1,0:T(8,128)(2,1)}, u32[]{:S(2)}, u32[]{:S(2)}) %collective-permute-start.11) | collective-permute-done | bytes 786464 | tf_op jit(solution)/shard_map/ppermute | solution.py:161
  172.5 16.2 %collective-permute-done.5 = bf16[128,3072]{1,0:T(8,128)(2,1)} collective-permute-done((bf16[128,3072]{1,0:T(8,128)(2,1)}, bf16[128,3072]{1,0:T(8,128)(2,1)}, u32[]{:S(2)}, u32[]{:S(2)}) %collective-permute-start.5) | collective-permute-done | bytes 786464 | tf_op jit(solution)/shard_map/ppermute | solution.py:159
  189.5 60.7 %all_gather.6 = s32[2048,64]{0,1:T(8,128)S(1)} all-gather(s32[128,64]{0,1:T(8,128)S(1)} %fusion.10), channel_id=1, replica_groups=mesh['grp'=2,'tok'=4,'feat'=4] {'tok','feat'}, dimensions={0}, use_global_device_ids=true | all-gather | bytes 557056 | tf_op jit(solution)/shard_map/all_gather | solution.py:152
  250.6 1.3 collective-permute-start.13
  251.9 1.3 collective-permute-start.7
  253.2 9.7 %select_reduce_fusion = s32[2048,64]{0,1:T(8,128)} fusion(s32[2048,64]{0,1:T(8,128)S(1)} %get-tuple-element.9, s32[2048,64]{0,1:T(8,128)S(1)} %get-tuple-element.8), kind=kLoop, calls=%fused_computation.1 | loop fusion | flops 25034752 | bytes 1572864 | tf_op jit(solution)/shard_map/reduce_sum | solution.py:136
  263.0 3.7 fusion.4
  266.7 3.4 collective-permute-done.13
  270.2 5.1 collective-permute-start.14
  275.3 11.7 %collective-permute-done.7 = bf16[128,3072]{1,0:T(8,128)(2,1)} collective-permute-done((bf16[128,3072]{1,0:T(8,128)(2,1)}, bf16[128,3072]{1,0:T(8,128)(2,1)}, u32[]{:S(2)}, u32[]{:S(2)}) %collective-permute-start.7) | collective-permute-done | bytes 786464 | tf_op jit(solution)/shard_map/ppermute | solution.py:159
  287.0 2.1 bitcast_dynamic-update-slice_fusion.15
  289.1 2.1 bitcast_dynamic-update-slice_fusion.14
  291.2 2.1 bitcast_dynamic-update-slice_fusion.13
  293.3 2.1 bitcast_dynamic-update-slice_fusion.12
  295.4 0.9 bitcast_dynamic-update-slice_fusion.11
  296.3 1.0 bitcast_dynamic-update-slice_fusion.10
  297.3 0.9 bitcast_dynamic-update-slice_fusion.9
  298.3 0.9 bitcast_dynamic-update-slice_fusion.8
  299.2 0.9 bitcast_dynamic-update-slice_fusion.7
  300.1 0.9 bitcast_dynamic-update-slice_fusion.6
  301.1 0.9 bitcast_dynamic-update-slice_fusion.5
  302.0 2.1 bitcast_dynamic-update-slice_fusion.4
  304.1 2.1 bitcast_dynamic-update-slice_fusion.3
  306.2 2.1 bitcast_dynamic-update-slice_fusion.2
  308.3 2.1 bitcast_dynamic-update-slice_fusion.1
  310.3 1.0 bitcast_dynamic-update-slice_fusion
  311.4 11.1 %gather_fusion = bf16[16,128,3072]{2,1,0:T(8,128)(2,1)} fusion(bf16[16,128,3072]{2,1,0:T(8,128)(2,1)} %bitcast_dynamic-update-slice_fusion, s32[1024]{0:T(1024)S(1)} %pad_clamp_fusion), kind=kCustom, calls=%fused_computation | custom fusion | bytes 25165888 | tf_op jit(solution)/shard_map/gather | solution.py:164
  322.4 10.0 %select_convert_fusion.1 = bf16[2048,512]{1,0:T(8,128)(2,1)S(1)} fusion(pred[2048,512]{1,0:T(32,128)(4,1)} %fusion.4, bf16[2048,3072]{1,0:T(8,128)(2,1)} %bitcast.45, bf16[3072,512]{1,0:T(8,128)(2,1)S(1)} %copy-done, f32[512]{0:T(512)S(1)} %copy-done.19), kind=kOutput, calls=%fused_computation.13 | convolution fusion | flops 6445596672 | bytes 18876416 | tf_op jit(solution)/shard_map/dot_general | solution.py:167
  332.4 1.3 copy-done.20
  333.7 9.6 %convolution_convert_fusion = bf16[2048,3072]{1,0:T(8,128)(2,1)} fusion(bf16[2048,512]{1,0:T(8,128)(2,1)S(1)} %select_convert_fusion.1, bf16[512,3072]{1,0:T(8,128)(2,1)S(1)} %copy-done.4), kind=kOutput, calls=%fused_computation.3 | convolution fusion | flops 6448742400 | bytes 17825792 | tf_op jit(solution)/shard_map/dot_general | solution.py:169
  343.4 135.0 %reduce-scatter.2.cloned.1.call-done = bf16[128,3072]{1,0:T(8,128)(2,1)} async-done(((bf16[2048,3072]{1,0:T(8,128)(2,1)}), bf16[128,3072]{1,0:T(8,128)(2,1)}) %reduce-scatter.2.cloned.1.call-update) | async-done | bytes 786448 | tf_op jit(solution)/shard_map/reduce_scatter | solution.py:172
  478.5 2.3 subtract_convert_fusion
  480.7 100.6 %all-gather.2.cloned.1.call-done = bf16[2048,3072]{1,0:T(8,128)(2,1)} async-done(((bf16[128,3072]{1,0:T(8,128)(2,1)}), bf16[2048,3072]{1,0:T(8,128)(2,1)}) %all-gather.2.cloned.1.call-update) | async-done | bytes 12582928 | tf_op jit(solution)/shard_map/all_gather | solution.py:176
  581.3 11.8 %fusion.1 = (f32[512]{0:T(512)S(1)}, f32[512]{0:T(512)S(1)}, f32[512,3072]{1,0:T(8,128)S(1)}) fusion(bf16[512,3072]{1,0:T(8,128)(2,1)} %param.12, bf16[2048,512]{1,0:T(8,128)(2,1)} %copy-done.20, bf16[2048,3072]{1,0:T(8,128)(2,1)} %all-gather.2.cloned.1.call-done), kind=kOutput, calls=%fused_computation.8 | convolution fusion | flops 6450314240 | bytes 24121344 | tf_op jit(solution)/shard_map/dot_general | solution.py:184
  593.1 3.1 fusion.3
  596.2 25.0 %convolution_convert_fusion.1 = bf16[3072,512]{1,0:T(8,128)(2,1)} fusion(bf16[2048,3072]{1,0:T(8,128)(2,1)} %bitcast.46, pred[2048,512]{1,0:T(32,128)(4,1)} %fusion.4, bf16[2048,3072]{1,0:T(8,128)(2,1)} %all-gather.2.cloned.1.call-done, bf16[512,3072]{1,0:T(8,128)(2,1)} %param.12), kind=kOutput, calls=%fused_computation.11 | convolution fusion | flops 12888571904 | bytes 32505856 | tf_op jit(solution)/shard_map/dot_general | solution.py:181
  (65 shorter events, 4.3 us)
Async XLA Ops:
  7.2 315.3 %copy-start = (bf16[3072,512]{1,0:T(8,128)(2,1)S(1)}, bf16[3072,512]{1,0:T(8,128)(2,1)}, u32[]{:S(2)}) copy-start(bf16[3072,512]{1,0:T(8,128)(2,1)} %param.10) | copy-start | bytes 9437188
  7.2 471.3 %reduce-scatter.2.cloned.1.call-start = ((), (), s32[]{:S(2)}) async-start(), calls=%async_computation.1 | async-start | bytes 13369344 | tf_op jit(solution)/shard_map/reduce_scatter | solution.py:172
  7.2 23.0 %collective-permute-start = (bf16[128,3072]{1,0:T(8,128)(2,1)}, bf16[128,3072]{1,0:T(8,128)(2,1)S(1)}, u32[]{:S(2)}, u32[]{:S(2)}) collective-permute-start(bf16[128,3072]{1,0:T(8,128)(2,1)} %param.7), channel_id=1, source_target_pairs={{0,1},{1,2},{2,3},{3,4},{4,5},{5,6},{6,7},{7,8},{8,9},{9,10},{10,1... | collective-permute-start | bytes 2359304 | tf_op jit(solution)/shard_map/ppermute | solution.py:159
  30.2 0.9 copy-start.6
  31.1 22.5 %collective-permute-start.1 = (bf16[128,3072]{1,0:T(8,128)(2,1)S(1)}, bf16[128,3072]{1,0:T(8,128)(2,1)S(1)}, u32[]{:S(2)}, u32[]{:S(2)}) collective-permute-start(bf16[128,3072]{1,0:T(8,128)(2,1)S(1)} %collective-permute-done), channel_id=1, source_target_pairs={{0,1},{1,2},{2,3},{3,4},{4,5},{5,6},{6,7},{7,8},{8,9},{9,10},{10,1... | collective-permute-start | bytes 2359304 | tf_op jit(solution)/shard_map/ppermute | solution.py:159
  31.1 36.6 %collective-permute-start.8 = (bf16[128,3072]{1,0:T(8,128)(2,1)}, bf16[128,3072]{1,0:T(8,128)(2,1)S(1)}, u32[]{:S(2)}, u32[]{:S(2)}) collective-permute-start(bf16[128,3072]{1,0:T(8,128)(2,1)} %param.7), channel_id=1, source_target_pairs={{1,0},{2,1},{3,2},{4,3},{5,4},{6,5},{7,6},{8,7},{9,8},{10,9},{11,1... | collective-permute-start | bytes 2359304 | tf_op jit(solution)/shard_map/ppermute | solution.py:161
  53.6 50.6 %copy-start.10 = (bf16[128,3072]{1,0:T(8,128)(2,1)}, bf16[128,3072]{1,0:T(8,128)(2,1)S(1)}, u32[]{:S(2)}) copy-start(bf16[128,3072]{1,0:T(8,128)(2,1)S(1)} %collective-permute-done.1) | copy-start | bytes 2359300
  53.6 33.8 %collective-permute-start.2 = (bf16[128,3072]{1,0:T(8,128)(2,1)S(1)}, bf16[128,3072]{1,0:T(8,128)(2,1)S(1)}, u32[]{:S(2)}, u32[]{:S(2)}) collective-permute-start(bf16[128,3072]{1,0:T(8,128)(2,1)S(1)} %collective-permute-done.1), channel_id=1, source_target_pairs={{0,1},{1,2},{2,3},{3,4},{4,5},{5,6},{6,7},{7,8},{8,9},{9,10},{10,1... | collective-permute-start | bytes 2359304 | tf_op jit(solution)/shard_map/ppermute | solution.py:159
  67.7 0.9 copy-start.8
  68.6 35.5 %collective-permute-start.9 = (bf16[128,3072]{1,0:T(8,128)(2,1)S(1)}, bf16[128,3072]{1,0:T(8,128)(2,1)S(1)}, u32[]{:S(2)}, u32[]{:S(2)}) collective-permute-start(bf16[128,3072]{1,0:T(8,128)(2,1)S(1)} %collective-permute-done.8), channel_id=1, source_target_pairs={{1,0},{2,1},{3,2},{4,3},{5,4},{6,5},{7,6},{8,7},{9,8},{10,9},{11,1... | collective-permute-start | bytes 2359304 | tf_op jit(solution)/shard_map/ppermute | solution.py:161
  87.4 51.4 %copy-start.14 = (bf16[128,3072]{1,0:T(8,128)(2,1)}, bf16[128,3072]{1,0:T(8,128)(2,1)S(1)}, u32[]{:S(2)}) copy-start(bf16[128,3072]{1,0:T(8,128)(2,1)S(1)} %collective-permute-done.2) | copy-start | bytes 2359300
  87.4 33.8 %collective-permute-start.3 = (bf16[128,3072]{1,0:T(8,128)(2,1)S(1)}, bf16[128,3072]{1,0:T(8,128)(2,1)S(1)}, u32[]{:S(2)}, u32[]{:S(2)}) collective-permute-start(bf16[128,3072]{1,0:T(8,128)(2,1)S(1)} %collective-permute-done.2), channel_id=1, source_target_pairs={{0,1},{1,2},{2,3},{3,4},{4,5},{5,6},{6,7},{7,8},{8,9},{9,10},{10,1... | collective-permute-start | bytes 2359304 | tf_op jit(solution)/shard_map/ppermute | solution.py:159
  104.2 0.9 copy-start.12
  104.2 34.6 %collective-permute-start.10 = (bf16[128,3072]{1,0:T(8,128)(2,1)S(1)}, bf16[128,3072]{1,0:T(8,128)(2,1)}, u32[]{:S(2)}, u32[]{:S(2)}) collective-permute-start(bf16[128,3072]{1,0:T(8,128)(2,1)S(1)} %collective-permute-done.9), channel_id=1, source_target_pairs={{1,0},{2,1},{3,2},{4,3},{5,4},{6,5},{7,6},{8,7},{9,8},{10,9},{11,1... | collective-permute-start | bytes 2359304 | tf_op jit(solution)/shard_map/ppermute | solution.py:161
  121.1 17.7 %copy-start.16 = (bf16[128,3072]{1,0:T(8,128)(2,1)}, bf16[128,3072]{1,0:T(8,128)(2,1)S(1)}, u32[]{:S(2)}) copy-start(bf16[128,3072]{1,0:T(8,128)(2,1)S(1)} %collective-permute-done.3) | copy-start | bytes 2359300
  121.1 33.9 %collective-permute-start.4 = (bf16[128,3072]{1,0:T(8,128)(2,1)S(1)}, bf16[128,3072]{1,0:T(8,128)(2,1)}, u32[]{:S(2)}, u32[]{:S(2)}) collective-permute-start(bf16[128,3072]{1,0:T(8,128)(2,1)S(1)} %collective-permute-done.3), channel_id=1, source_target_pairs={{0,1},{1,2},{2,3},{3,4},{4,5},{5,6},{6,7},{7,8},{8,9},{9,10},{10,1... | collective-permute-start | bytes 2359304 | tf_op jit(solution)/shard_map/ppermute | solution.py:159
  138.8 33.7 %collective-permute-start.11 = (bf16[128,3072]{1,0:T(8,128)(2,1)}, bf16[128,3072]{1,0:T(8,128)(2,1)}, u32[]{:S(2)}, u32[]{:S(2)}) collective-permute-start(bf16[128,3072]{1,0:T(8,128)(2,1)} %collective-permute-done.10), channel_id=1, source_target_pairs={{1,0},{2,1},{3,2},{4,3},{5,4},{6,5},{7,6},{8,7},{9,8},{10,9},{11,1... | collective-permute-start | bytes 2359304 | tf_op jit(solution)/shard_map/ppermute | solution.py:161
  155.0 33.7 %collective-permute-start.5 = (bf16[128,3072]{1,0:T(8,128)(2,1)}, bf16[128,3072]{1,0:T(8,128)(2,1)}, u32[]{:S(2)}, u32[]{:S(2)}) collective-permute-start(bf16[128,3072]{1,0:T(8,128)(2,1)} %collective-permute-done.4), channel_id=1, source_target_pairs={{0,1},{1,2},{2,3},{3,4},{4,5},{5,6},{6,7},{7,8},{8,9},{9,10},{10,1... | collective-permute-start | bytes 2359304 | tf_op jit(solution)/shard_map/ppermute | solution.py:159
  172.5 78.1 %collective-permute-start.12 = (bf16[128,3072]{1,0:T(8,128)(2,1)}, bf16[128,3072]{1,0:T(8,128)(2,1)}, u32[]{:S(2)}, u32[]{:S(2)}) collective-permute-start(bf16[128,3072]{1,0:T(8,128)(2,1)} %collective-permute-done.11), channel_id=1, source_target_pairs={{1,0},{2,1},{3,2},{4,3},{5,4},{6,5},{7,6},{8,7},{9,8},{10,9},{11,1... | collective-permute-start | bytes 2359304 | tf_op jit(solution)/shard_map/ppermute | solution.py:161
  188.7 63.2 %collective-permute-start.6 = (bf16[128,3072]{1,0:T(8,128)(2,1)}, bf16[128,3072]{1,0:T(8,128)(2,1)}, u32[]{:S(2)}, u32[]{:S(2)}) collective-permute-start(bf16[128,3072]{1,0:T(8,128)(2,1)} %collective-permute-done.5), channel_id=1, source_target_pairs={{0,1},{1,2},{2,3},{3,4},{4,5},{5,6},{6,7},{7,8},{8,9},{9,10},{10,1... | collective-permute-start | bytes 2359304 | tf_op jit(solution)/shard_map/ppermute | solution.py:159
  250.6 19.5 %collective-permute-start.13 = (bf16[128,3072]{1,0:T(8,128)(2,1)}, bf16[128,3072]{1,0:T(8,128)(2,1)}, u32[]{:S(2)}, u32[]{:S(2)}) collective-permute-start(bf16[128,3072]{1,0:T(8,128)(2,1)} %collective-permute-done.12), channel_id=1, source_target_pairs={{1,0},{2,1},{3,2},{4,3},{5,4},{6,5},{7,6},{8,7},{9,8},{10,9},{11,1... | collective-permute-start | bytes 2359304 | tf_op jit(solution)/shard_map/ppermute | solution.py:161
  251.9 35.1 %collective-permute-start.7 = (bf16[128,3072]{1,0:T(8,128)(2,1)}, bf16[128,3072]{1,0:T(8,128)(2,1)}, u32[]{:S(2)}, u32[]{:S(2)}) collective-permute-start(bf16[128,3072]{1,0:T(8,128)(2,1)} %collective-permute-done.6), channel_id=1, source_target_pairs={{0,1},{1,2},{2,3},{3,4},{4,5},{5,6},{6,7},{7,8},{8,9},{9,10},{10,1... | collective-permute-start | bytes 2359304 | tf_op jit(solution)/shard_map/ppermute | solution.py:159
  262.9 32.5 %copy-start.17 = (bf16[128,3072]{1,0:T(8,128)(2,1)S(1)}, bf16[128,3072]{1,0:T(8,128)(2,1)}, u32[]{:S(2)}) copy-start(bf16[128,3072]{1,0:T(8,128)(2,1)} %copy-done.16) | copy-start | bytes 2359300
  262.9 33.4 %copy-start.15 = (bf16[128,3072]{1,0:T(8,128)(2,1)S(1)}, bf16[128,3072]{1,0:T(8,128)(2,1)}, u32[]{:S(2)}) copy-start(bf16[128,3072]{1,0:T(8,128)(2,1)} %copy-done.14) | copy-start | bytes 2359300
  262.9 34.4 %copy-start.11 = (bf16[128,3072]{1,0:T(8,128)(2,1)S(1)}, bf16[128,3072]{1,0:T(8,128)(2,1)}, u32[]{:S(2)}) copy-start(bf16[128,3072]{1,0:T(8,128)(2,1)} %copy-done.10) | copy-start | bytes 2359300
  262.9 35.3 %copy-start.7 = (bf16[128,3072]{1,0:T(8,128)(2,1)S(1)}, bf16[128,3072]{1,0:T(8,128)(2,1)}, u32[]{:S(2)}) copy-start(bf16[128,3072]{1,0:T(8,128)(2,1)} %copy-done.6) | copy-start | bytes 2359300
  262.9 36.3 %copy-start.2 = (bf16[128,3072]{1,0:T(8,128)(2,1)S(1)}, bf16[128,3072]{1,0:T(8,128)(2,1)}, u32[]{:S(2)}) copy-start(bf16[128,3072]{1,0:T(8,128)(2,1)} %param.7) | copy-start | bytes 2359300
  262.9 37.2 %copy-start.9 = (bf16[128,3072]{1,0:T(8,128)(2,1)S(1)}, bf16[128,3072]{1,0:T(8,128)(2,1)}, u32[]{:S(2)}) copy-start(bf16[128,3072]{1,0:T(8,128)(2,1)} %copy-done.8) | copy-start | bytes 2359300
  263.0 38.1 %copy-start.13 = (bf16[128,3072]{1,0:T(8,128)(2,1)S(1)}, bf16[128,3072]{1,0:T(8,128)(2,1)}, u32[]{:S(2)}) copy-start(bf16[128,3072]{1,0:T(8,128)(2,1)} %copy-done.12) | copy-start | bytes 2359300
  270.2 40.2 %collective-permute-start.14 = (bf16[128,3072]{1,0:T(8,128)(2,1)}, bf16[128,3072]{1,0:T(8,128)(2,1)S(1)}, u32[]{:S(2)}, u32[]{:S(2)}) collective-permute-start(bf16[128,3072]{1,0:T(8,128)(2,1)} %collective-permute-done.13), channel_id=1, source_target_pairs={{1,0},{2,1},{3,2},{4,3},{5,4},{6,5},{7,6},{8,7},{9,8},{10,9},{11,1... | collective-permute-start | bytes 2359304 | tf_op jit(solution)/shard_map/ppermute | solution.py:161
  311.4 11.1 %copy-start.19 = (f32[512]{0:T(512)S(1)}, f32[512]{0:T(512)}, u32[]{:S(2)}) copy-start(f32[512]{0:T(512)} %param.11) | copy-start | bytes 6148
  322.4 11.3 %copy-start.4 = (bf16[512,3072]{1,0:T(8,128)(2,1)S(1)}, bf16[512,3072]{1,0:T(8,128)(2,1)}, u32[]{:S(2)}) copy-start(bf16[512,3072]{1,0:T(8,128)(2,1)} %param.12) | copy-start | bytes 9437188
  332.4 1.3 copy-start.20
  343.3 135.1 %copy-start.3 = (bf16[128,3072]{1,0:T(8,128)(2,1)S(1)}, bf16[128,3072]{1,0:T(8,128)(2,1)}, u32[]{:S(2)}) copy-start(bf16[128,3072]{1,0:T(8,128)(2,1)} %param.7) | copy-start | bytes 2359300
  343.3 135.1 %copy-start.18 = (f32[3072]{0:T(1024)S(1)}, f32[3072]{0:T(1024)}, u32[]{:S(2)}) copy-start(f32[3072]{0:T(1024)} %param.13) | copy-start | bytes 36868
  343.4 237.9 %all-gather.2.cloned.1.call-start = ((), (), s32[]{:S(2)}) async-start(), calls=%async_computation.2 | async-start | bytes 13369344 | tf_op jit(solution)/shard_map/all_gather | solution.py:176
  480.7 112.4 %copy-start.5 = (bf16[512,3072]{1,0:T(8,128)(2,1)S(1)}, bf16[512,3072]{1,0:T(8,128)(2,1)}, u32[]{:S(2)}) copy-start(bf16[512,3072]{1,0:T(8,128)(2,1)} %param.12) | copy-start | bytes 9437188
  596.2 25.0 %copy-start.1 = (bf16[3072,512]{1,0:T(8,128)(2,1)S(1)}, bf16[3072,512]{1,0:T(8,128)(2,1)}, u32[]{:S(2)}) copy-start(bf16[3072,512]{1,0:T(8,128)(2,1)} %param.10) | copy-start | bytes 9437188
Sparse Core Ops, SparseCore 0:
  343.5 134.9 reduce-scatter.1
  481.3 99.9 all-gather.1
